TPU v7x, 256 devices: a whole 4x4x8 slice. The times are simulated.
256 devices in a mesh: ctx: 16 (over y_hi, x, core), dp: 16 (over y_lo, z).
Axes of the slice: x: 4, y: 4 (y_hi: 2, y_lo: 2; y = y_hi * 2 + y_lo), z: 8, core: 2. Of those that a mesh axis runs over, the one named last changes fastest.
Arguments:
- queries: bfloat16 [16, 2048, 1536], P('dp', 'ctx'), as said below
- keys: bfloat16 [16, 2048, 1536], P('dp', 'ctx'), as said below
- values: bfloat16 [16, 2048, 1536], P('dp', 'ctx'), may hold values from -6 to 6
- tangent_queries: bfloat16 [16, 2048, 1536], P('dp', 'ctx'), may hold values from -6 to 6
- tangent_keys: bfloat16 [16, 2048, 1536], P('dp', 'ctx'), may hold values from -6 to 6
- tangent_values: bfloat16 [16, 2048, 1536], P('dp', 'ctx'), may hold values from -6 to 6
- clip_ids: int32 [16, 2048], P('dp', 'ctx'), may hold values from 0 to 3, never falling along the last dimension, each value on 1 to 1024 neighbouring positions
- block_order: int32 [16], replicated, may hold values from 0 to 15, each once
- out_weight: bfloat16 [1536, 3072], replicated, may hold values from -0.15625 to 0.15625
- layer_scale: float32 [3072], replicated, may hold values from 0.1 to 1.9
- cotangent: bfloat16 [16, 2048, 3072], P('dp', 'ctx'), as said below
Outputs:
- tangent_branch: bfloat16 [16, 2048, 3072], P('dp', 'ctx')
- scale_grad: float32 [3072], replicated
Inputs may be any that keep to these rules, and one draw needn't show every extreme that they name: `clip_ids`: ids never fall along a sample's rows; each of the 4 clips is a run of consecutive rows. `block_order`: each block number appears once. `queries`: real-valued. `keys`: real-valued. `cotangent`: real-valued.
All inputs are finite; a program needn't handle non-finite values.
Results may differ from a plain program's by a relative error of at most 0.02.
The roundings to bfloat16 on the way count: a program that leaves them out, or rounds other values in their place, can miss the bound.
Values may be sent and summed in bfloat16 or wider, within the bound.
A program may use at most 192 MiB of HBM per device.

v0:
```python
import math
import jax
import jax.numpy as jnp
from jax import lax
from jax.sharding import PartitionSpec as P

HEADS = 12


def rotate(x, pos, half_dim):
    frequency = 10000.0 ** (-jnp.arange(half_dim, dtype=jnp.float32) / half_dim)
    angles = pos.astype(jnp.float32)[:, None] * frequency[None, :]
    cosine = jnp.cos(angles)[:, None, :]
    sine_part = jnp.sin(angles)[:, None, :]
    front_part = x[..., :half_dim]
    back_part = x[..., half_dim:]
    return jnp.concatenate(
        [front_part * cosine - back_part * sine_part, back_part * cosine + front_part * sine_part],
        axis=-1,
    )


def make_attend(query_rot, tquery_rot, query_ids, scale):

    def attend(carry, block):
        best, total, weighted, primal_acc, slope_acc, spread_acc = carry
        key_blk, value_blk, tkey_blk, tvalue_blk, key_ids = block
        scores = (
            jnp.einsum("hqd,hkd->hqk", query_rot, key_blk, preferred_element_type=jnp.float32)
            * scale
        )
        same_clip = query_ids[:, None] == key_ids[None, :]
        scores = jnp.where(same_clip[None], scores, -jnp.inf)
        slopes = (
            jnp.einsum("hqd,hkd->hqk", tquery_rot, key_blk, preferred_element_type=jnp.float32)
            + jnp.einsum("hqd,hkd->hqk", query_rot, tkey_blk, preferred_element_type=jnp.float32)
        ) * scale
        new_best = jnp.maximum(best, jnp.max(scores, axis=-1))
        factor = jnp.exp(best - new_best)
        weights = jnp.exp(scores - new_best[..., None])
        tilted = weights * slopes
        total = total * factor + jnp.sum(weights, axis=-1)
        weighted = weighted * factor + jnp.sum(tilted, axis=-1)
        weights_b = weights.astype(jnp.bfloat16)
        tilted_b = tilted.astype(jnp.bfloat16)
        primal_acc = primal_acc * factor[..., None] + jnp.einsum(
            "hqk,hkd->hqd", weights_b, value_blk, preferred_element_type=jnp.float32
        )
        slope_acc = slope_acc * factor[..., None] + jnp.einsum(
            "hqk,hkd->hqd", tilted_b, value_blk, preferred_element_type=jnp.float32
        )
        spread_acc = spread_acc * factor[..., None] + jnp.einsum(
            "hqk,hkd->hqd", weights_b, tvalue_blk, preferred_element_type=jnp.float32
        )
        return ((new_best, total, weighted, primal_acc, slope_acc, spread_acc), None)

    return attend


def start_states(heads, rows, head_dim):
    zeros_rows = jnp.zeros((heads, rows), jnp.float32)
    zeros_heads = jnp.zeros((heads, rows, head_dim), jnp.float32)
    return (
        jnp.full((heads, rows), -1e30, jnp.float32),
        zeros_rows,
        zeros_rows,
        zeros_heads,
        zeros_heads,
        zeros_heads,
    )


def local(
    queries,
    keys,
    values,
    tangent_queries,
    tangent_keys,
    tangent_values,
    clip_ids,
    block_order,
    out_weight,
    layer_scale,
    cotangent,
):
    tok_rows = queries.shape[1]
    heads = HEADS
    head_dim = queries.shape[2] // heads
    scale = head_dim ** (-0.5)
    cycle_index = lax.axis_index("ctx")
    positions = block_order[cycle_index] * tok_rows + jnp.arange(tok_rows, dtype=jnp.int32)

    def heads_first(x, turned):
        y = x[0].reshape(tok_rows, heads, head_dim)
        if turned:
            y = rotate(y.astype(jnp.float32), positions, head_dim // 2).astype(jnp.bfloat16)
        return jnp.transpose(y, (1, 0, 2))

    query_rot = heads_first(queries, True)
    key_rot = heads_first(keys, True)
    value_heads = heads_first(values, False)
    tquery_rot = heads_first(tangent_queries, True)
    tkey_rot = heads_first(tangent_keys, True)
    tvalue_heads = heads_first(tangent_values, False)
    all_ids = lax.all_gather(clip_ids, "ctx", axis=1, tiled=True)[0]
    own_ids = clip_ids[0]
    attend = make_attend(query_rot, tquery_rot, own_ids, scale)
    carry = start_states(heads, tok_rows, head_dim)
    key_part = lax.all_gather(key_rot, "ctx", axis=1, tiled=True)
    value_part = lax.all_gather(value_heads, "ctx", axis=1, tiled=True)
    tkey_part = lax.all_gather(tkey_rot, "ctx", axis=1, tiled=True)
    tvalue_part = lax.all_gather(tvalue_heads, "ctx", axis=1, tiled=True)
    count = key_part.shape[1]
    block_rows = math.gcd(count, tok_rows)
    blocks = count // block_rows

    def split_blocks(x):
        return jnp.transpose(x.reshape(heads, blocks, block_rows, head_dim), (1, 0, 2, 3))

    stacked = (
        split_blocks(key_part),
        split_blocks(value_part),
        split_blocks(tkey_part),
        split_blocks(tvalue_part),
        all_ids.reshape(blocks, block_rows),
    )
    carry, unused = lax.scan(attend, carry, stacked)
    best, total, weighted, primal_acc, slope_acc, spread_acc = carry
    mean_out = primal_acc / total[..., None]
    tangent_heads = (
        (slope_acc + spread_acc) / total[..., None] - (weighted / total)[..., None] * mean_out
    ).astype(jnp.bfloat16)
    tangent_rows = jnp.transpose(tangent_heads, (1, 0, 2)).reshape(tok_rows, heads * head_dim)
    projected = jnp.dot(tangent_rows, out_weight, preferred_element_type=jnp.float32)
    branch = (layer_scale * projected).astype(jnp.bfloat16)[None]
    partial_grad = jnp.sum(cotangent[0].astype(jnp.float32) * projected, axis=0)
    summed = lax.psum(partial_grad, ("ctx", "dp"))
    count_all = lax.axis_size("ctx") * lax.axis_size("dp") * tok_rows
    return (branch, summed / math.sqrt(count_all))


def solution(mesh):
    in_specs = (
        P("dp", "ctx", None),
        P("dp", "ctx", None),
        P("dp", "ctx", None),
        P("dp", "ctx", None),
        P("dp", "ctx", None),
        P("dp", "ctx", None),
        P("dp", "ctx"),
        P(),
        P(),
        P(),
        P("dp", "ctx", None),
    )
    out_specs = (P("dp", "ctx", None), P())
    return jax.shard_map(local, mesh=mesh, in_specs=in_specs, out_specs=out_specs, check_vma=False)
```

profile of v0, /device:TPU:1, one launch (start us, length us, event | category | flops | bytes accessed | tf_op | source)
XLA Modules:
  0.0 623.5 jit_solution(16415383374081786712)
XLA Ops:
  18.6 1.9 copy.28
  22.8 25.8 %all_gather.15 = s32[1,2048]{1,0:T(1,128)} all-gather(s32[1,128]{1,0:T(1,128)} %param.19), channel_id=1, replica_groups=mesh['ctx'=16,'dp'=16] {'ctx'}, dimensions={1}, use_global_device_ids=true | all-gather | bytes 8704 | tf_op jit(solution)/shard_map/all_gather | solution.py:105
  48.7 46.9 %all-gather.5.cloned.1.call-done = bf16[12,2048,128]{1,2,0:T(8,128)(2,1)} async-done(((bf16[12,128,128]{1,2,0:T(8,128)(2,1)}), bf16[12,2048,128]{1,2,0:T(8,128)(2,1)}) %all-gather.5.cloned.1.call-update) | async-done | bytes 6291472 | tf_op jit(solution)/shard_map/all_gather | solution.py:109
  95.6 7.8 %copy.44 = bf16[192,8,16,128]{3,2,1,0:T(8,128)(2,1)} copy(bf16[192,8,16,128]{3,1,2,0:T(8,128)(2,1)} %bitcast.120) | data formatting | bytes 12582912
  103.3 9.0 %copy.21 = bf16[12,16,128,128]{3,2,0,1:T(8,128)(2,1)} copy(bf16[12,16,128,128]{2,1,3,0:T(8,128)(2,1)} %bitcast.115) | data formatting | bytes 12582912 | tf_op jit(solution)/shard_map/reshape | solution.py:118
  112.4 58.9 %all-gather.7.cloned.1.call-done = bf16[12,2048,128]{1,2,0:T(8,128)(2,1)} async-done(((bf16[12,128,128]{1,2,0:T(8,128)(2,1)}), bf16[12,2048,128]{1,2,0:T(8,128)(2,1)}) %all-gather.7.cloned.1.call-update) | async-done | bytes 6291472 | tf_op jit(solution)/shard_map/all_gather | solution.py:111
  171.3 8.7 %copy.25 = bf16[12,2048,128]{2,1,0:T(8,128)(2,1)} copy(bf16[12,2048,128]{1,2,0:T(8,128)(2,1)} %all-gather.7.cloned.1.call-done) | data formatting | bytes 12582912 | tf_op jit(solution)/shard_map/all_gather | solution.py:111
  180.0 67.1 %all-gather.9.cloned.1.call-done = bf16[12,2048,128]{1,2,0:T(8,128)(2,1)} async-done(((bf16[12,128,128]{1,2,0:T(8,128)(2,1)}), bf16[12,2048,128]{1,2,0:T(8,128)(2,1)}) %all-gather.9.cloned.1.call-update) | async-done | bytes 6291472 | tf_op jit(solution)/shard_map/all_gather | solution.py:110
  247.1 8.6 %copy.27 = bf16[12,2048,128]{2,1,0:T(8,128)(2,1)} copy(bf16[12,2048,128]{1,2,0:T(8,128)(2,1)} %all-gather.9.cloned.1.call-done) | data formatting | bytes 12582912 | tf_op jit(solution)/shard_map/all_gather | solution.py:110
  255.7 67.0 %all-gather.11.cloned.1.call-done = bf16[12,2048,128]{1,2,0:T(8,128)(2,1)} async-done(((bf16[12,128,128]{1,2,0:T(8,128)(2,1)}), bf16[12,2048,128]{1,2,0:T(8,128)(2,1)}) %all-gather.11.cloned.1.call-update) | async-done | bytes 6291472 | tf_op jit(solution)/shard_map/all_gather | solution.py:112
  322.7 8.7 %copy.29 = bf16[12,2048,128]{2,1,0:T(8,128)(2,1)} copy(bf16[12,2048,128]{1,2,0:T(8,128)(2,1)} %all-gather.11.cloned.1.call-done) | data formatting | bytes 12582912 | tf_op jit(solution)/shard_map/all_gather | solution.py:112
  331.3 200.5 %while.21 = (s32[]{:T(128)}, f32[12,128]{1,0:T(8,128)S(1)}, f32[12,128]{1,0:T(8,128)}, f32[12,128]{1,0:T(8,128)}, f32[12,128,128]{2,1,0:T(8,128)S(1)}, /*index=5...) while((s32[]{:T(128)}, f32[12,128]{1,0:T(8,128)S(1)}, ...), condition=%wide.region_4.5_spmd.clone, body=%wide.region_0.4_spmd.clone.sunk | while | flops 306735616 | bytes 14789864 | solution.py:127
  337.8 1.6 convolution_add_fusion.9
  339.3 1.6 convolution_add_fusion.8
  340.9 1.6 convolution_add_fusion.7
  350.3 1.6 convolution_add_fusion.9
  351.9 1.6 convolution_add_fusion.8
  353.5 1.6 convolution_add_fusion.7
  362.9 1.6 convolution_add_fusion.9
  364.5 1.6 convolution_add_fusion.8
  366.0 1.6 convolution_add_fusion.7
  375.5 1.6 convolution_add_fusion.9
  377.0 1.6 convolution_add_fusion.8
  378.6 1.6 convolution_add_fusion.7
  388.1 1.6 convolution_add_fusion.9
  389.6 1.6 convolution_add_fusion.8
  391.2 1.6 convolution_add_fusion.7
  400.6 1.6 convolution_add_fusion.9
  402.2 1.6 convolution_add_fusion.8
  403.8 1.6 convolution_add_fusion.7
  413.2 1.6 convolution_add_fusion.9
  414.8 1.6 convolution_add_fusion.8
  416.3 1.6 convolution_add_fusion.7
  425.8 1.6 convolution_add_fusion.9
  427.4 1.6 convolution_add_fusion.8
  428.9 1.6 convolution_add_fusion.7
  438.4 1.6 convolution_add_fusion.9
  439.9 1.6 convolution_add_fusion.8
  441.5 1.6 convolution_add_fusion.7
  450.9 1.6 convolution_add_fusion.9
  452.5 1.6 convolution_add_fusion.8
  454.1 1.6 convolution_add_fusion.7
  463.5 1.6 convolution_add_fusion.9
  465.1 1.6 convolution_add_fusion.8
  466.6 1.6 convolution_add_fusion.7
  476.1 1.6 convolution_add_fusion.9
  477.6 1.6 convolution_add_fusion.8
  479.2 1.6 convolution_add_fusion.7
  484.4 1.5 fusion.72
  488.6 1.6 convolution_add_fusion.9
  490.2 1.6 convolution_add_fusion.8
  491.8 1.6 convolution_add_fusion.7
  501.2 1.6 convolution_add_fusion.9
  502.8 1.6 convolution_add_fusion.8
  504.3 1.6 convolution_add_fusion.7
  513.8 1.6 convolution_add_fusion.9
  515.3 1.6 convolution_add_fusion.8
  516.9 1.6 convolution_add_fusion.7
  522.1 1.5 fusion.72
  526.4 1.6 convolution_add_fusion.9
  527.9 1.6 convolution_add_fusion.8
  529.5 1.6 convolution_add_fusion.7
  534.3 6.4 %fusion.32 = (f32[3072]{0:T(1024)S(1)}, bf16[1,128,3072]{2,1,0:T(8,128)(2,1)}) fusion(bf16[1,128,3072]{2,1,0:T(8,128)(2,1)} %param.23, f32[3072]{0:T(1024)S(1)} %copy-done.3, bf16[128,1536]{0,1:T(8,128)(2,1)S(1)} %bitcast.121, bf16[1536,3072]{1,0:T(8,128)(2,1)} %param.21), kind=kOutput, calls=%fused_computation.46 | convolution fusion | flops 1209922560 | bytes 11427840 | tf_op jit(solution)/shard_map/dot_general | solution.py:134
  540.7 75.7 %psum.7 = f32[3072]{0:T(1024)S(1)} all-reduce(f32[3072]{0:T(1024)S(1)} %get-tuple-element.187), channel_id=1, replica_groups=mesh['ctx'=16,'dp'=16] {'ctx','dp'}, use_global_device_ids=true, to_apply=%region_6.7 | all-reduce | flops 3072 | bytes 24576 | tf_op jit(solution)/shard_map/psum | solution.py:137
  (265 shorter events, 136.7 us)
Async XLA Ops:
  7.2 88.4 %all-gather.5.cloned.1.call-start = ((), (), s32[]{:S(2)}) async-start(), calls=%async_computation | async-start | bytes 6684672 | tf_op jit(solution)/shard_map/all_gather | solution.py:109
  11.7 5.9 copy-start.2
  16.6 154.7 %all-gather.7.cloned.1.call-start = ((), (), s32[]{:S(2)}) async-start(), calls=%async_computation.1 | async-start | bytes 6684672 | tf_op jit(solution)/shard_map/all_gather | solution.py:111
  17.5 229.6 %all-gather.9.cloned.1.call-start = ((), (), s32[]{:S(2)}) async-start(), calls=%async_computation.2 | async-start | bytes 6684672 | tf_op jit(solution)/shard_map/all_gather | solution.py:110
  18.5 304.1 %all-gather.11.cloned.1.call-start = ((), (), s32[]{:S(2)}) async-start(), calls=%async_computation.3 | async-start | bytes 6684672 | tf_op jit(solution)/shard_map/all_gather | solution.py:112
  334.2 8.4 %copy-start = (f32[12,128]{1,0:T(8,128)S(1)}, f32[12,128]{1,0:T(8,128)}, u32[]{:S(2)}) copy-start(f32[12,128]{1,0:T(8,128)} %get-tuple-element.331) | copy-start | bytes 18436 | tf_op jit(solution)/shard_map/while
  342.6 0.6 copy-start.1
  346.1 9.1 %copy-start = (f32[12,128]{1,0:T(8,128)S(1)}, f32[12,128]{1,0:T(8,128)}, u32[]{:S(2)}) copy-start(f32[12,128]{1,0:T(8,128)} %get-tuple-element.331) | copy-start | bytes 18436 | tf_op jit(solution)/shard_map/while
  355.2 0.6 copy-start.1
  358.6 9.1 %copy-start = (f32[12,128]{1,0:T(8,128)S(1)}, f32[12,128]{1,0:T(8,128)}, u32[]{:S(2)}) copy-start(f32[12,128]{1,0:T(8,128)} %get-tuple-element.331) | copy-start | bytes 18436 | tf_op jit(solution)/shard_map/while
  367.8 0.6 copy-start.1
  371.2 9.1 %copy-start = (f32[12,128]{1,0:T(8,128)S(1)}, f32[12,128]{1,0:T(8,128)}, u32[]{:S(2)}) copy-start(f32[12,128]{1,0:T(8,128)} %get-tuple-element.331) | copy-start | bytes 18436 | tf_op jit(solution)/shard_map/while
  380.3 0.6 copy-start.1
  383.8 9.1 %copy-start = (f32[12,128]{1,0:T(8,128)S(1)}, f32[12,128]{1,0:T(8,128)}, u32[]{:S(2)}) copy-start(f32[12,128]{1,0:T(8,128)} %get-tuple-element.331) | copy-start | bytes 18436 | tf_op jit(solution)/shard_map/while
  392.9 0.6 copy-start.1
  396.4 9.1 %copy-start = (f32[12,128]{1,0:T(8,128)S(1)}, f32[12,128]{1,0:T(8,128)}, u32[]{:S(2)}) copy-start(f32[12,128]{1,0:T(8,128)} %get-tuple-element.331) | copy-start | bytes 18436 | tf_op jit(solution)/shard_map/while
  405.5 0.6 copy-start.1
  408.9 9.1 %copy-start = (f32[12,128]{1,0:T(8,128)S(1)}, f32[12,128]{1,0:T(8,128)}, u32[]{:S(2)}) copy-start(f32[12,128]{1,0:T(8,128)} %get-tuple-element.331) | copy-start | bytes 18436 | tf_op jit(solution)/shard_map/while
  418.1 0.6 copy-start.1
  421.5 9.1 %copy-start = (f32[12,128]{1,0:T(8,128)S(1)}, f32[12,128]{1,0:T(8,128)}, u32[]{:S(2)}) copy-start(f32[12,128]{1,0:T(8,128)} %get-tuple-element.331) | copy-start | bytes 18436 | tf_op jit(solution)/shard_map/while
  430.6 0.6 copy-start.1
  434.1 9.1 %copy-start = (f32[12,128]{1,0:T(8,128)S(1)}, f32[12,128]{1,0:T(8,128)}, u32[]{:S(2)}) copy-start(f32[12,128]{1,0:T(8,128)} %get-tuple-element.331) | copy-start | bytes 18436 | tf_op jit(solution)/shard_map/while
  443.2 0.6 copy-start.1
  446.7 9.1 %copy-start = (f32[12,128]{1,0:T(8,128)S(1)}, f32[12,128]{1,0:T(8,128)}, u32[]{:S(2)}) copy-start(f32[12,128]{1,0:T(8,128)} %get-tuple-element.331) | copy-start | bytes 18436 | tf_op jit(solution)/shard_map/while
  455.8 0.6 copy-start.1
  459.2 9.1 %copy-start = (f32[12,128]{1,0:T(8,128)S(1)}, f32[12,128]{1,0:T(8,128)}, u32[]{:S(2)}) copy-start(f32[12,128]{1,0:T(8,128)} %get-tuple-element.331) | copy-start | bytes 18436 | tf_op jit(solution)/shard_map/while
  468.4 0.6 copy-start.1
  471.8 9.1 %copy-start = (f32[12,128]{1,0:T(8,128)S(1)}, f32[12,128]{1,0:T(8,128)}, u32[]{:S(2)}) copy-start(f32[12,128]{1,0:T(8,128)} %get-tuple-element.331) | copy-start | bytes 18436 | tf_op jit(solution)/shard_map/while
  480.9 0.6 copy-start.1
  484.4 9.1 %copy-start = (f32[12,128]{1,0:T(8,128)S(1)}, f32[12,128]{1,0:T(8,128)}, u32[]{:S(2)}) copy-start(f32[12,128]{1,0:T(8,128)} %get-tuple-element.331) | copy-start | bytes 18436 | tf_op jit(solution)/shard_map/while
  493.5 0.6 copy-start.1
  496.9 9.1 %copy-start = (f32[12,128]{1,0:T(8,128)S(1)}, f32[12,128]{1,0:T(8,128)}, u32[]{:S(2)}) copy-start(f32[12,128]{1,0:T(8,128)} %get-tuple-element.331) | copy-start | bytes 18436 | tf_op jit(solution)/shard_map/while
  506.1 0.6 copy-start.1
  509.5 9.1 %copy-start = (f32[12,128]{1,0:T(8,128)S(1)}, f32[12,128]{1,0:T(8,128)}, u32[]{:S(2)}) copy-start(f32[12,128]{1,0:T(8,128)} %get-tuple-element.331) | copy-start | bytes 18436 | tf_op jit(solution)/shard_map/while
  518.6 0.6 copy-start.1
  522.1 9.1 %copy-start = (f32[12,128]{1,0:T(8,128)S(1)}, f32[12,128]{1,0:T(8,128)}, u32[]{:S(2)}) copy-start(f32[12,128]{1,0:T(8,128)} %get-tuple-element.331) | copy-start | bytes 18436 | tf_op jit(solution)/shard_map/while
  531.2 0.6 copy-start.1
  531.8 2.5 copy-start.3
Sparse Core Ops, SparseCore 0:
  16.7 78.7 all-gather.4
  98.1 73.1 all-gather.6
  173.9 73.1 all-gather.8
  249.5 73.1 all-gather.10
where the time goes:
time: 630 us; the launch traced here: 623 us
  waiting for transfers between devices  240 us (38%)
  matrix products  150 us (24%)
  blocking collectives  102 us (16%)
  local copies, waits for them, and re-layouts  74 us (12%)
  other arithmetic  41 us (7%)
  between operations  14.6 us (2%)
    psum x1, blocking collectives, local(): summed = lax.psum(partial_grad, ('ctx', 'dp'))  75.7 us
    all_gather x1, waiting for transfers between devices, local(): value_part = lax.all_gather(value_heads, 'ctx', axis=1, tiled=True)  67.1 us
    all_gather x1, waiting for transfers between devices, local(): tvalue_part = lax.all_gather(tvalue_heads, 'ctx', axis=1, tiled=True)  67 us
    all_gather x1, waiting for transfers between devices, local(): tkey_part = lax.all_gather(tkey_rot, 'ctx', axis=1, tiled=True)  58.9 us
    all_gather x1, waiting for transfers between devices, local(): key_part = lax.all_gather(key_rot, 'ctx', axis=1, tiled=True)  46.9 us
    all_gather x1, blocking collectives, local(): all_ids = lax.all_gather(clip_ids, 'ctx', axis=1, tiled=True)[0]  25.8 us
    dot_general x16, matrix products, attend(): jnp.einsum('hqk,hkd->hqd', weights_b, value_blk, preferred_element_type=j...  25.1 us
    dot_general x16, matrix products, attend(): jnp.einsum('hqk,hkd->hqd', tilted_b, value_blk, preferred_element_type=jn...  24.9 us
  transfers between devices with their start and end apart: 4, of which 4 were waited for; matrix products, arithmetic and copies ran while one was open for 6% of the time, Pallas kernels for 0%

commit v1 on v0

--- a/solution.py
+++ b/solution.py
@@ -134,7 +134,7 @@
     projected = jnp.dot(tangent_rows, out_weight, preferred_element_type=jnp.float32)
     branch = (layer_scale * projected).astype(jnp.bfloat16)[None]
     partial_grad = jnp.sum(cotangent[0].astype(jnp.float32) * projected, axis=0)
-    summed = lax.psum(partial_grad, ("ctx", "dp"))
+    summed = jnp.sum(lax.all_gather(partial_grad, ("ctx", "dp")), axis=0)
     count_all = lax.axis_size("ctx") * lax.axis_size("dp") * tok_rows
     return (branch, summed / math.sqrt(count_all))
 

time: 630 us -> 1260 us (2.00)
  waiting for transfers between devices: 240 us -> 942 us
  blocking collectives: 102 us -> 26.4 us
    all_gather x0 -> x1, waiting for transfers between devices: none -> 702 us  [local(): summed = jnp.sum(lax.all_gather(partial_grad, ('ctx', 'dp')), axis=0)]
    psum x1 -> x0, blocking collectives: 75.7 us -> none  [local(): summed = lax.psum(partial_grad, ('ctx', 'dp'))]
  transfers between devices with their start and end apart: 4 -> 5, of which waited for: 4 -> 5; matrix products, arithmetic and copies ran while one was open for 6% -> 3% of each run, Pallas kernels for 0% -> 0%
where the time goes in v1:
time: 1260 us; the launch traced here: 1250 us
  waiting for transfers between devices  942 us (75%)
  matrix products  151 us (12%)
  local copies, waits for them, and re-layouts  77 us (6%)
  other arithmetic  41.2 us (3%)
  blocking collectives  26.4 us (2%)
  between operations  14.6 us (1%)
    all_gather x1, waiting for transfers between devices, local(): summed = jnp.sum(lax.all_gather(partial_grad, ('ctx', 'dp')), axis=0)  702 us
    all_gather x1, waiting for transfers between devices, local(): value_part = lax.all_gather(value_heads, 'ctx', axis=1, tiled=True)  67.1 us
    all_gather x1, waiting for transfers between devices, local(): tvalue_part = lax.all_gather(tvalue_heads, 'ctx', axis=1, tiled=True)  67 us
    all_gather x1, waiting for transfers between devices, local(): tkey_part = lax.all_gather(tkey_rot, 'ctx', axis=1, tiled=True)  59 us
    all_gather x1, waiting for transfers between devices, local(): key_part = lax.all_gather(key_rot, 'ctx', axis=1, tiled=True)  46.2 us
    all_gather x1, blocking collectives, local(): all_ids = lax.all_gather(clip_ids, 'ctx', axis=1, tiled=True)[0]  26.4 us
  transfers between devices with their start and end apart: 5, of which 5 were waited for; matrix products, arithmetic and copies ran while one was open for 3% of the time, Pallas kernels for 0%

profile of v1, /device:TPU:1, one launch (start us, length us, event | category | flops | bytes accessed | tf_op | source)
XLA Modules:
  0.0 1254.0 jit_solution(17240583803942315129)
XLA Ops:
  18.6 1.9 copy.70
  22.9 26.4 %all_gather.21 = s32[1,2048]{1,0:T(1,128)} all-gather(s32[1,128]{1,0:T(1,128)} %param.19), channel_id=1, replica_groups=mesh['ctx'=16,'dp'=16] {'ctx'}, dimensions={1}, use_global_device_ids=true | all-gather | bytes 8704 | tf_op jit(solution)/shard_map/all_gather | solution.py:105
  49.4 46.2 %all-gather.7.cloned.1.call-done = bf16[12,2048,128]{1,2,0:T(8,128)(2,1)} async-done(((bf16[12,128,128]{1,2,0:T(8,128)(2,1)}), bf16[12,2048,128]{1,2,0:T(8,128)(2,1)}) %all-gather.7.cloned.1.call-update) | async-done | bytes 6291472 | tf_op jit(solution)/shard_map/all_gather | solution.py:109
  95.6 7.8 copy.86
  103.3 9.0 copy.63
  112.3 59.0 %all-gather.9.cloned.1.call-done = bf16[12,2048,128]{1,2,0:T(8,128)(2,1)} async-done(((bf16[12,128,128]{1,2,0:T(8,128)(2,1)}), bf16[12,2048,128]{1,2,0:T(8,128)(2,1)}) %all-gather.9.cloned.1.call-update) | async-done | bytes 6291472 | tf_op jit(solution)/shard_map/all_gather | solution.py:111
  171.3 8.7 copy.67
  180.0 67.1 %all-gather.11.cloned.1.call-done = bf16[12,2048,128]{1,2,0:T(8,128)(2,1)} async-done(((bf16[12,128,128]{1,2,0:T(8,128)(2,1)}), bf16[12,2048,128]{1,2,0:T(8,128)(2,1)}) %all-gather.11.cloned.1.call-update) | async-done | bytes 6291472 | tf_op jit(solution)/shard_map/all_gather | solution.py:110
  247.1 8.6 copy.69
  255.7 67.0 %all-gather.13.cloned.1.call-done = bf16[12,2048,128]{1,2,0:T(8,128)(2,1)} async-done(((bf16[12,128,128]{1,2,0:T(8,128)(2,1)}), bf16[12,2048,128]{1,2,0:T(8,128)(2,1)}) %all-gather.13.cloned.1.call-update) | async-done | bytes 6291472 | tf_op jit(solution)/shard_map/all_gather | solution.py:112
  322.7 8.7 copy.71
  331.4 200.7 %while.21 = (s32[]{:T(128)}, f32[12,128]{1,0:T(8,128)S(1)}, f32[12,128]{1,0:T(8,128)}, f32[12,128]{1,0:T(8,128)}, f32[12,128,128]{2,1,0:T(8,128)S(1)}, /*index=5...) while((s32[]{:T(128)}, f32[12,128]{1,0:T(8,128)S(1)}, ...), condition=%wide.region_4.5_spmd.clone, body=%wide.region_0.4_spmd.clone.sunk | while | flops 306735616 | bytes 14789864 | solution.py:127
  337.8 1.6 convolution_add_fusion.9
  339.4 1.6 convolution_add_fusion.8
  340.9 1.6 convolution_add_fusion.7
  346.1 1.5 fusion.72
  350.4 1.6 convolution_add_fusion.9
  351.9 1.6 convolution_add_fusion.8
  353.5 1.6 convolution_add_fusion.7
  363.0 1.6 convolution_add_fusion.9
  364.5 1.6 convolution_add_fusion.8
  366.1 1.6 convolution_add_fusion.7
  375.6 1.6 convolution_add_fusion.9
  377.1 1.6 convolution_add_fusion.8
  378.7 1.6 convolution_add_fusion.7
  388.1 1.6 convolution_add_fusion.9
  389.7 1.6 convolution_add_fusion.8
  391.3 1.6 convolution_add_fusion.7
  400.7 1.6 convolution_add_fusion.9
  402.3 1.6 convolution_add_fusion.8
  403.8 1.6 convolution_add_fusion.7
  413.3 1.6 convolution_add_fusion.9
  414.9 1.6 convolution_add_fusion.8
  416.4 1.6 convolution_add_fusion.7
  425.9 1.6 convolution_add_fusion.9
  427.4 1.6 convolution_add_fusion.8
  429.0 1.6 convolution_add_fusion.7
  438.5 1.6 convolution_add_fusion.9
  440.0 1.6 convolution_add_fusion.8
  441.6 1.6 convolution_add_fusion.7
  451.1 1.6 convolution_add_fusion.9
  452.6 1.6 convolution_add_fusion.8
  454.2 1.6 convolution_add_fusion.7
  463.6 1.6 convolution_add_fusion.9
  465.2 1.6 convolution_add_fusion.8
  466.8 1.6 convolution_add_fusion.7
  476.2 1.6 convolution_add_fusion.9
  477.8 1.6 convolution_add_fusion.8
  479.3 1.6 convolution_add_fusion.7
  488.8 1.6 convolution_add_fusion.9
  490.4 1.6 convolution_add_fusion.8
  491.9 1.6 convolution_add_fusion.7
  501.4 1.6 convolution_add_fusion.9
  503.0 1.6 convolution_add_fusion.8
  504.5 1.6 convolution_add_fusion.7
  514.0 1.6 convolution_add_fusion.9
  515.5 1.6 convolution_add_fusion.8
  517.1 1.6 convolution_add_fusion.7
  526.6 1.6 convolution_add_fusion.9
  528.1 1.6 convolution_add_fusion.8
  529.7 1.6 convolution_add_fusion.7
  534.5 7.0 fusion.32
  541.5 702.4 %all-gather.15.cloned.1.call-done = f32[786432]{0:T(1024)} async-done(((f32[3072]{0:T(1024)}), f32[786432]{0:T(1024)}) %all-gather.15.cloned.1.call-update) | async-done | bytes 3145744 | tf_op jit(solution)/shard_map/all_gather | solution.py:137
  1243.9 2.8 reshape.134
  (269 shorter events, 138.7 us)
Async XLA Ops:
  7.2 88.4 %all-gather.7.cloned.1.call-start = ((), (), s32[]{:S(2)}) async-start(), calls=%async_computation | async-start | bytes 6684672 | tf_op jit(solution)/shard_map/all_gather | solution.py:109
  11.7 5.9 copy-start.2
  16.6 154.7 %all-gather.9.cloned.1.call-start = ((), (), s32[]{:S(2)}) async-start(), calls=%async_computation.1 | async-start | bytes 6684672 | tf_op jit(solution)/shard_map/all_gather | solution.py:111
  17.5 229.5 %all-gather.11.cloned.1.call-start = ((), (), s32[]{:S(2)}) async-start(), calls=%async_computation.2 | async-start | bytes 6684672 | tf_op jit(solution)/shard_map/all_gather | solution.py:110
  18.5 304.1 %all-gather.13.cloned.1.call-start = ((), (), s32[]{:S(2)}) async-start(), calls=%async_computation.3 | async-start | bytes 6684672 | tf_op jit(solution)/shard_map/all_gather | solution.py:112
  20.5 1223.3 %all-gather.15.cloned.1.call-start = ((), (), s32[]{:S(2)}) async-start(), calls=%async_computation.4 | async-start | bytes 3158016 | tf_op jit(solution)/shard_map/all_gather | solution.py:137
  334.2 8.4 copy-start
  342.7 0.6 copy-start.1
  346.1 9.1 copy-start
  355.2 0.6 copy-start.1
  358.7 9.1 copy-start
  367.8 0.6 copy-start.1
  371.3 9.1 copy-start
  380.4 0.6 copy-start.1
  383.9 9.1 copy-start
  393.0 0.6 copy-start.1
  396.4 9.1 copy-start
  405.6 0.6 copy-start.1
  409.0 9.1 copy-start
  418.2 0.6 copy-start.1
  421.6 9.1 copy-start
  430.7 0.6 copy-start.1
  434.2 9.1 copy-start
  443.3 0.6 copy-start.1
  446.8 9.1 copy-start
  455.9 0.6 copy-start.1
  459.4 9.1 copy-start
  468.5 0.6 copy-start.1
  472.0 9.1 copy-start
  481.1 0.6 copy-start.1
  484.5 9.1 copy-start
  493.7 0.6 copy-start.1
  497.1 9.1 copy-start
  506.3 0.6 copy-start.1
  509.7 9.1 copy-start
  518.8 0.6 copy-start.1
  522.3 9.1 copy-start
  531.4 0.6 copy-start.1
  532.0 2.5 copy-start.3
Sparse Core Ops, SparseCore 0:
  16.7 78.7 all-gather.6
  98.1 73.1 all-gather.8
  173.9 73.1 all-gather.10
  249.5 73.1 all-gather.12
  541.6 702.1 all-gather.14
